TPU v7x, 32 devices: a whole 2x2x4 slice. The times are simulated.
32 devices in a mesh: row: 8 (over z, core), rep: 4 (over y, x).
Axes of the slice: x: 2, y: 2, z: 4, core: 2. Of those that a mesh axis runs over, the one named last changes fastest.
Arguments:
- features: bfloat16 [4096, 256], P(('row', 'rep')), may hold values from -6 to 6
- weight: bfloat16 [256, 256], replicated, may hold values from -0.375 to 0.375
- cotangent: bfloat16 [4096, 256], P(('row', 'rep')), may hold values from -6 to 6
- adjacency: bfloat16 [8, 4, 24, 128, 128], P('row', 'rep'), may hold values from -0.15625 to 0.15625
- tile_out: int32 [8, 4, 24], P('row', 'rep'), may hold values from 0 to 3
- tile_in: int32 [8, 4, 24], P('row', 'rep'), may hold values from 0 to 7
- live_count: int32 [8, 4], P('row', 'rep'), may hold values from 6 to 24, as said below
Outputs:
- activated: bfloat16 [4096, 256], P(('row', 'rep'))
- weight_grad: float32 [256, 256], replicated
- feature_grad: float32 [4096, 256], P(('row', 'rep'))
Inputs may be any that keep to these rules, and one draw needn't show every extreme that they name: `live_count`: live tile slots of one device; some device has all 24 slots live in every draw.
All inputs are finite; a program needn't handle non-finite values.
Results may differ from a plain program's by a relative error of at most 0.02.
Values may be sent and summed in bfloat16 or wider, within the bound.
A program may use at most 64 MiB of HBM per device.

v0:
```python
import math
import jax
import jax.numpy as jnp
from jax import lax
from jax.sharding import PartitionSpec as P


def tile_sums(adjacency, first_ids, second_ids, live_mask, table, count, transpose_tile):
    slot_count = adjacency.shape[0]
    block_rows = adjacency.shape[1]
    feat_width = table.shape[2]
    group_size = math.gcd(slot_count, 8)
    turns = slot_count // group_size
    items = (
        adjacency.reshape(turns, group_size, block_rows, block_rows),
        first_ids.reshape(turns, group_size),
        second_ids.reshape(turns, group_size),
        live_mask.reshape(turns, group_size),
    )

    def step_group(running, item):
        tile_group, read_ids, write_ids, live_group = item
        inputs = table[read_ids]
        if transpose_tile:
            products = jnp.einsum(
                "gji,gjf->gif", tile_group, inputs, preferred_element_type=jnp.float32
            )
        else:
            products = jnp.einsum(
                "gij,gjf->gif", tile_group, inputs, preferred_element_type=jnp.float32
            )
        onehot = (write_ids[None, :] == jnp.arange(count)[:, None]).astype(
            jnp.float32
        ) * live_group[None, :]
        running = running + jnp.einsum(
            "bg,gif->bif", onehot, products, precision=lax.Precision.HIGHEST
        )
        return (running, None)

    start = jnp.zeros((count, block_rows, feat_width), jnp.float32)
    running, unused = lax.scan(step_group, start, items)
    return running.reshape(count * block_rows, feat_width)


def add_sources(received):
    return jnp.sum(received.astype(jnp.float32), axis=0)


def body(features, weight, cotangent, adjacency, tile_out, tile_in, live_count):
    block_rows = features.shape[0]
    feat_width = features.shape[1]
    row_count = lax.axis_size("row")
    rep_count = lax.axis_size("rep")
    slot_count = adjacency.shape[2]
    adjacency = adjacency.reshape(slot_count, block_rows, block_rows)
    out_ids = tile_out.reshape(slot_count)
    in_ids = tile_in.reshape(slot_count)
    live_mask = (jnp.arange(slot_count) < live_count.reshape(())).astype(jnp.float32)
    gathered = lax.all_gather(features, "row", axis=0, tiled=True).reshape(
        row_count, block_rows, feat_width
    )
    partial_value = tile_sums(adjacency, in_ids, out_ids, live_mask, gathered, rep_count, False)
    aggregated = lax.psum_scatter(
        partial_value.astype(jnp.bfloat16), "rep", scatter_dimension=0, tiled=True
    )
    pre = jnp.dot(aggregated, weight, preferred_element_type=jnp.float32)
    sig = jax.nn.sigmoid(pre)
    activated = (pre * sig).astype(jnp.bfloat16)
    grad_pre = (cotangent.astype(jnp.float32) * sig * (1.0 + pre * (1.0 - sig))).astype(
        jnp.bfloat16
    )
    weight_part = jnp.dot(aggregated.T, grad_pre, preferred_element_type=jnp.float32)
    grad_rows = jnp.dot(grad_pre, weight.T, preferred_element_type=jnp.float32).astype(jnp.bfloat16)
    group_grads = lax.all_gather(grad_rows, "rep", axis=0, tiled=True)
    weight_grad = lax.psum(weight_part, ("row", "rep"))
    group_grads = group_grads.reshape(rep_count, block_rows, feat_width)
    returned = tile_sums(adjacency, out_ids, in_ids, live_mask, group_grads, row_count, True)
    rounded = returned.astype(jnp.bfloat16).reshape(row_count, block_rows, feat_width)
    feature_grad = add_sources(
        lax.all_to_all(rounded, "row", split_axis=0, concat_axis=0, tiled=True)
    )
    return (activated, weight_grad, feature_grad)


def solution(mesh):
    return jax.shard_map(
        body,
        mesh=mesh,
        in_specs=(
            P(("row", "rep"), None),
            P(),
            P(("row", "rep"), None),
            P("row", "rep", None, None, None),
            P("row", "rep", None),
            P("row", "rep", None),
            P("row", "rep"),
        ),
        out_specs=(P(("row", "rep"), None), P(), P(("row", "rep"), None)),
        check_vma=False,
    )
```

profile of v0, /device:TPU:0, one launch (start us, length us, event | category | flops | bytes accessed | tf_op | source)
XLA Modules:
  0.0 231.4 jit_solution(6620039171133740857)
XLA Ops:
  7.9 0.5 broadcast.99
  8.6 0.7 reduce.6
  9.3 0.7 reduce.7
  10.1 16.7 %all_gather.6 = bf16[1024,256]{1,0:T(8,128)(2,1)S(1)} all-gather(bf16[128,256]{1,0:T(8,128)(2,1)} %param.11), channel_id=1, replica_groups=mesh['row'=8,'rep'=4] {'row'}, dimensions={0}, use_global_device_ids=true | all-gather | bytes 589824 | tf_op jit(solution)/shard_map/all_gather | solution.py:59
  26.8 10.8 %while.22 = (s32[]{:T(128)}, f32[4,128,256]{2,0,1:T(4,128)S(1)}, s32[3,8]{1,0:T(4,128)S(1)}, f32[3,8]{1,0:T(4,128)S(1)}, bf16[3,8,128,128]{3,2,1,0:T(8,128)(2,1)...) while((s32[]{:T(128)}, f32[4,128,256]{2,0,1:T(4,128)S(1)}, ...), condition=%wide.region_1.2_spmd.clone, body=%wide.region_0.1_spmd.clone.sunk | while | flops 79955032 | bytes 4985279 | solution.py:41
  26.8 0.6 gather_fusion
  27.4 1.2 fusion.61
  28.7 1.7 convolution_add_fusion.4
  30.5 0.6 gather_fusion
  31.0 1.2 fusion.61
  32.3 1.7 convolution_add_fusion.4
  34.1 0.6 gather_fusion
  34.7 1.2 fusion.61
  35.9 1.7 convolution_add_fusion.4
  37.6 0.8 copy.25
  39.2 24.8 %reduce-scatter.2.cloned.1.call-done = bf16[128,256]{1,0:T(8,128)(2,1)} async-done(((bf16[512,256]{1,0:T(8,128)(2,1)}), bf16[128,256]{1,0:T(8,128)(2,1)}) %reduce-scatter.2.cloned.1.call-update) | async-done | bytes 65552 | tf_op jit(solution)/shard_map/reduce_scatter | solution.py:63
  64.0 1.7 multiply_convert_fusion
  65.9 9.3 %all_gather.7 = bf16[512,256]{1,0:T(8,128)(2,1)S(1)} all-gather(bf16[128,256]{1,0:T(8,128)(2,1)S(1)} %convolution_convert_fusion), channel_id=1, replica_groups=mesh['row'=8,'rep'=4] {'rep'}, dimensions={0}, use_global_device_ids=true | all-gather | bytes 327680 | tf_op jit(solution)/shard_map/all_gather | solution.py:74
  75.2 7.9 %while.23 = (s32[]{:T(128)}, f32[8,128,256]{2,0,1:T(8,128)S(1)}, s32[3,8]{1,0:T(4,128)S(1)}, f32[3,8]{1,0:T(4,128)S(1)}, bf16[3,8,128,128]{2,3,1,0:T(8,128)(2,1)...) while((s32[]{:T(128)}, f32[8,128,256]{2,0,1:T(8,128)S(1)}, ...), condition=%wide.region_5.6_spmd.clone, body=%wide.region_4.5_spmd.clone.sunk | while | flops 92800152 | bytes 6033855 | solution.py:41
  75.3 0.6 gather_fusion.1
  76.1 1.7 convolution_add_fusion.5
  77.9 0.6 gather_fusion.1
  78.8 1.7 convolution_add_fusion.5
  80.6 0.6 gather_fusion.1
  81.4 1.7 convolution_add_fusion.5
  83.1 1.1 copy.24
  84.2 4.8 %all-to-all-start = ((bf16[8,128,256]{2,1,0:T(8,128)(2,1)}), bf16[8,128,256]{2,1,0:T(8,128)(2,1)S(1)}, u32[]{:S(2)}, u32[]{:S(2)}) async-start(bf16[8,128,256]{2,1,0:T(8,128)(2,1)} %copy.24), calls=%async_computation.1 | async-start | bytes 1048576 | tf_op jit(solution)/shard_map/all_to_all | solution.py:80
  89.0 0.9 fusion.31
  90.0 14.4 %all-to-all-done = bf16[8,128,256]{2,1,0:T(8,128)(2,1)S(1)} async-done(((bf16[8,128,256]{2,1,0:T(8,128)(2,1)}), bf16[8,128,256]{2,1,0:T(8,128)(2,1)S(1)}, u32[]{:S(2)}, u32[]{:S(2)}) %all-to-all-start) | async-done | bytes 524320 | tf_op jit(solution)/shard_map/all_to_all | solution.py:80
  104.3 0.7 convert_reduce_fusion
  105.1 117.8 %all-reduce.2.cloned.1.call-done = f32[256,256]{1,0:T(8,128)} async-done(((f32[256,256]{1,0:T(8,128)}), f32[256,256]{1,0:T(8,128)}) %all-reduce.2.cloned.1.call-update) | async-done | bytes 262160 | tf_op jit(solution)/shard_map/psum | solution.py:75
  222.9 1.7 copy.44
  (50 shorter events, 2.5 us)
Async XLA Ops:
  7.2 56.8 %copy-start = (bf16[256,256]{1,0:T(8,128)(2,1)S(1)}, bf16[256,256]{1,0:T(8,128)(2,1)}, u32[]{:S(2)}) copy-start(bf16[256,256]{1,0:T(8,128)(2,1)} %param.12) | copy-start | bytes 393220
  7.2 56.8 %reduce-scatter.2.cloned.1.call-start = ((), (), s32[]{:S(2)}) async-start(), calls=%async_computation.2 | async-start | bytes 327680 | tf_op jit(solution)/shard_map/reduce_scatter | solution.py:63
  7.9 0.7 copy-start.4
  8.6 0.7 copy-start.5
  37.6 1.2 copy-start.1
  38.8 25.2 %copy-start.3 = (bf16[128,256]{1,0:T(8,128)(2,1)S(1)}, bf16[128,256]{1,0:T(8,128)(2,1)}, u32[]{:S(2)}) copy-start(bf16[128,256]{1,0:T(8,128)(2,1)} %param.13) | copy-start | bytes 196612
  84.2 4.8 %copy-start.2 = (bf16[128,256]{1,0:T(8,128)(2,1)S(1)}, bf16[128,256]{1,0:T(8,128)(2,1)}, u32[]{:S(2)}) copy-start(bf16[128,256]{1,0:T(8,128)(2,1)} %reduce-scatter.2.cloned.1.call-done) | copy-start | bytes 196612
  84.2 20.1 %all-to-all-start = ((bf16[8,128,256]{2,1,0:T(8,128)(2,1)}), bf16[8,128,256]{2,1,0:T(8,128)(2,1)S(1)}, u32[]{:S(2)}, u32[]{:S(2)}) async-start(bf16[8,128,256]{2,1,0:T(8,128)(2,1)} %copy.24), calls=%async_computation.1 | async-start | bytes 1048576 | tf_op jit(solution)/shard_map/all_to_all | solution.py:80
  89.0 133.9 %all-reduce.2.cloned.1.call-start = ((), (), s32[]{:S(2)}) async-start(), calls=%async_computation.3 | async-start | bytes 524288 | tf_op jit(solution)/shard_map/psum | solution.py:75
Sparse Core Ops, SparseCore 0:
  38.5 25.4 reduce-scatter.1
  95.9 126.9 all-reduce.1
where the time goes:
time: 232 us; the launch traced here: 231 us
  waiting for transfers between devices  157 us (68%)
  blocking collectives  26 us (11%)
  matrix products  17.5 us (8%)
  between operations  14.8 us (6%)
  local copies, waits for them, and re-layouts  8.77 us (4%)
  starting transfers between devices  4.83 us (2%)
    psum x1, waiting for transfers between devices, body(): weight_grad = lax.psum(weight_part, ('row', 'rep'))  118 us
    reduce_scatter x1, waiting for transfers between devices, body(): lax.psum_scatter(partial_value.astype(jnp.bfloat16), 'rep', scatter_dimen...  24.8 us
    all_gather x1, blocking collectives, body(): lax.all_gather(features, 'row', axis=0, tiled=True)  16.7 us
    all_to_all x1, waiting for transfers between devices, body(): lax.all_to_all(rounded, 'row', split_axis=0, concat_axis=0, tiled=True)  14.4 us
    dot_general x6, matrix products, step_group(): jnp.einsum('bg,gif->bif', onehot, products, precision=lax.Precision.HIGHEST)  10.2 us
    all_gather x1, blocking collectives, body(): group_grads = lax.all_gather(grad_rows, 'rep', axis=0, tiled=True)  9.29 us
    all_to_all x1, starting transfers between devices, body(): lax.all_to_all(rounded, 'row', split_axis=0, concat_axis=0, tiled=True)  4.75 us
  transfers between devices with their start and end apart: 3, of which 3 were waited for; matrix products, arithmetic and copies ran while one was open for 1% of the time, Pallas kernels for 0%

commit v1 on v0

--- a/solution.py
+++ b/solution.py
@@ -72,7 +72,7 @@
     weight_part = jnp.dot(aggregated.T, grad_pre, preferred_element_type=jnp.float32)
     grad_rows = jnp.dot(grad_pre, weight.T, preferred_element_type=jnp.float32).astype(jnp.bfloat16)
     group_grads = lax.all_gather(grad_rows, "rep", axis=0, tiled=True)
-    weight_grad = lax.psum(weight_part, ("row", "rep"))
+    weight_grad = jnp.sum(lax.all_gather(weight_part, ("row", "rep")), axis=0)
     group_grads = group_grads.reshape(rep_count, block_rows, feat_width)
     returned = tile_sums(adjacency, out_ids, in_ids, live_mask, group_grads, row_count, True)
     rounded = returned.astype(jnp.bfloat16).reshape(row_count, block_rows, feat_width)

time: 232 us -> 166 us (0.72)
  waiting for transfers between devices: 157 us -> 58.4 us
  blocking collectives: 26 us -> 55 us
  other arithmetic: 2.17 us -> 8.09 us
  starting transfers between devices: 4.83 us -> 0.08 us
  matrix products: 17.5 us -> 21.2 us
    psum x1 -> x0, waiting for transfers between devices: 118 us -> none  [body(): weight_grad = lax.psum(weight_part, ('row', 'rep'))]
    all_gather x0 -> x1, waiting for transfers between devices: none -> 32.9 us  [body(): weight_grad = jnp.sum(lax.all_gather(weight_part, ('row', 'rep')), axis=0)]
    all_to_all x0 -> x1, blocking collectives: none -> 28.2 us  [body(): lax.all_to_all(rounded, 'row', split_axis=0, concat_axis=0, tiled=True)]
    all_to_all x1 -> x0, waiting for transfers between devices: 14.4 us -> none  [body(): lax.all_to_all(rounded, 'row', split_axis=0, concat_axis=0, tiled=True)]
    all_to_all x1 -> x0, starting transfers between devices: 4.75 us -> none  [body(): lax.all_to_all(rounded, 'row', split_axis=0, concat_axis=0, tiled=True)]
    reduce_sum x0 -> x1, other arithmetic: none -> 4.63 us  [body(): weight_grad = jnp.sum(lax.all_gather(weight_part, ('row', 'rep')), axis=0)]
    dot_general x3, matrix products: 0.85 us -> 3.71 us  [step_group(): jnp.einsum('gji,gjf->gif', tile_group, inputs, preferred_element_type=jnp...]
  transfers between devices with their start and end apart: 3 -> 2, of which waited for: 3 -> 2; matrix products, arithmetic and copies ran while one was open for 1% -> 9% of each run, Pallas kernels for 0% -> 0%
where the time goes in v1:
time: 166 us
  waiting for transfers between devices  58.4 us (35%)
  blocking collectives  55 us (33%)
  matrix products  21.2 us (13%)
  between operations  14.8 us (9%)
  other arithmetic  8.09 us (5%)
  local copies, waits for them, and re-layouts  7.7 us (5%)
    all_gather x1, waiting for transfers between devices, body(): weight_grad = jnp.sum(lax.all_gather(weight_part, ('row', 'rep')), axis=0)  32.9 us
    all_to_all x1, blocking collectives, body(): lax.all_to_all(rounded, 'row', split_axis=0, concat_axis=0, tiled=True)  28.2 us
    reduce_scatter x1, waiting for transfers between devices, body(): lax.psum_scatter(partial_value.astype(jnp.bfloat16), 'rep', scatter_dimen...  25.5 us
    all_gather x1, blocking collectives, body(): lax.all_gather(features, 'row', axis=0, tiled=True)  16.7 us
    dot_general x6, matrix products, step_group(): jnp.einsum('bg,gif->bif', onehot, products, precision=lax.Precision.HIGHEST)  10.2 us
    all_gather x1, blocking collectives, body(): group_grads = lax.all_gather(grad_rows, 'rep', axis=0, tiled=True)  10.1 us
    reduce_sum x1, other arithmetic, body(): weight_grad = jnp.sum(lax.all_gather(weight_part, ('row', 'rep')), axis=0)  4.63 us
    dot_general x3, matrix products, step_group(): jnp.einsum('gji,gjf->gif', tile_group, inputs, preferred_element_type=jnp...  3.71 us
  transfers between devices with their start and end apart: 2, of which 2 were waited for; matrix products, arithmetic and copies ran while one was open for 9% of the time, Pallas kernels for 0%

profile of v1, /device:TPU:0, one launch (start us, length us, event | category | flops | bytes accessed | tf_op | source)
XLA Modules:
  0.0 165.6 jit_solution(10340019128990848478)
XLA Ops:
  7.7 1.3 reduce.6
  9.8 1.3 reduce.7
  11.2 16.7 %all_gather.12 = bf16[1024,256]{1,0:T(8,128)(2,1)S(1)} all-gather(bf16[128,256]{1,0:T(8,128)(2,1)} %param.11), channel_id=1, replica_groups=mesh['row'=8,'rep'=4] {'row'}, dimensions={0}, use_global_device_ids=true | all-gather | bytes 589824 | tf_op jit(solution)/shard_map/all_gather | solution.py:59
  27.9 10.8 %while.22 = (s32[]{:T(128)}, f32[4,128,256]{2,0,1:T(4,128)S(1)}, s32[3,8]{1,0:T(4,128)S(1)}, f32[3,8]{1,0:T(4,128)S(1)}, bf16[3,8,128,128]{3,2,1,0:T(8,128)(2,1)...) while((s32[]{:T(128)}, f32[4,128,256]{2,0,1:T(4,128)S(1)}, ...), condition=%wide.region_1.2_spmd.clone, body=%wide.region_0.1_spmd.clone.sunk | while | flops 79955032 | bytes 4985279 | solution.py:41
  27.9 0.6 gather_fusion
  28.5 1.2 fusion.61
  29.8 1.7 %convolution_add_fusion.4 = f32[4,128,256]{2,0,1:T(4,128)S(1)} fusion(f32[8,128,256]{2,1,0:T(8,128)S(1)} %fusion.61, f32[4,128,256]{2,0,1:T(4,128)S(1)} %get-tuple-element.260, pred[]{:T(512)S(6)} %compare.6, f32[8]{0:T(128)S(1)} %fusion.62, s32[8]{0:T(128)S(1)} %fusion.63), kind=kOutput, calls=%fused_computation.2.clone.1 | convolution fusion | flops 12845120 | bytes 2097217 | tf_op jit(solution)/shard_map/while/body/eval_jaxpr/bg,gif->bif/dot_general | solution.py:35
  31.6 0.6 gather_fusion
  32.1 1.2 fusion.61
  33.4 1.7 %convolution_add_fusion.4 = f32[4,128,256]{2,0,1:T(4,128)S(1)} fusion(f32[8,128,256]{2,1,0:T(8,128)S(1)} %fusion.61, f32[4,128,256]{2,0,1:T(4,128)S(1)} %get-tuple-element.260, pred[]{:T(512)S(6)} %compare.6, f32[8]{0:T(128)S(1)} %fusion.62, s32[8]{0:T(128)S(1)} %fusion.63), kind=kOutput, calls=%fused_computation.2.clone.1 | convolution fusion | flops 12845120 | bytes 2097217 | tf_op jit(solution)/shard_map/while/body/eval_jaxpr/bg,gif->bif/dot_general | solution.py:35
  35.2 0.6 gather_fusion
  35.8 1.2 fusion.61
  37.0 1.7 %convolution_add_fusion.4 = f32[4,128,256]{2,0,1:T(4,128)S(1)} fusion(f32[8,128,256]{2,1,0:T(8,128)S(1)} %fusion.61, f32[4,128,256]{2,0,1:T(4,128)S(1)} %get-tuple-element.260, pred[]{:T(512)S(6)} %compare.6, f32[8]{0:T(128)S(1)} %fusion.62, s32[8]{0:T(128)S(1)} %fusion.63), kind=kOutput, calls=%fused_computation.2.clone.1 | convolution fusion | flops 12845120 | bytes 2097217 | tf_op jit(solution)/shard_map/while/body/eval_jaxpr/bg,gif->bif/dot_general | solution.py:35
  38.7 0.8 copy.25
  39.6 25.5 %reduce-scatter.2.cloned.1.call-done = bf16[128,256]{1,0:T(8,128)(2,1)} async-done(((bf16[512,256]{1,0:T(8,128)(2,1)}), bf16[128,256]{1,0:T(8,128)(2,1)}) %reduce-scatter.2.cloned.1.call-update) | async-done | bytes 65552 | tf_op jit(solution)/shard_map/reduce_scatter | solution.py:63
  65.1 1.7 %multiply_convert_fusion = (bf16[128,256]{1,0:T(8,128)(2,1)S(1)}, bf16[128,256]{1,0:T(8,128)(2,1)}) fusion(bf16[128,256]{1,0:T(8,128)(2,1)S(1)} %copy-done.1, bf16[128,256]{1,0:T(8,128)(2,1)} %reduce-scatter.2.cloned.1.call-done, bf16[256,256]{1,0:T(8,128)(2,1)S(1)} %copy-done), kind=kOutput, calls=%fused_computation.50 | convolution fusion | flops 17170432 | bytes 393216 | tf_op jit(solution)/shard_map/dot_general | solution.py:66
  66.8 1.8 %fusion.31 = f32[256,256]{1,0:T(8,128)} fusion(bf16[128,256]{1,0:T(8,128)(2,1)} %reduce-scatter.2.cloned.1.call-done, bf16[128,256]{1,0:T(8,128)(2,1)S(1)} %get-tuple-element.162), kind=kOutput, calls=%fused_computation.55 | convolution fusion | flops 16777216 | bytes 393216 | tf_op jit(solution)/shard_map/dot_general | solution.py:72
  68.6 2.3 %copy.13 = bf16[1,1,24,128,128]{3,4,2,1,0:T(8,128)(2,1)} copy(bf16[1,1,24,128,128]{4,3,2,1,0:T(8,128)(2,1)} %bitcast.84) | data formatting | bytes 1572864 | tf_op args[3]
  71.1 10.1 %all_gather.15 = bf16[512,256]{1,0:T(8,128)(2,1)S(1)} all-gather(bf16[128,256]{1,0:T(8,128)(2,1)S(1)} %convolution_convert_fusion), channel_id=1, replica_groups=mesh['row'=8,'rep'=4] {'rep'}, dimensions={0}, use_global_device_ids=true | all-gather | bytes 327680 | tf_op jit(solution)/shard_map/all_gather | solution.py:74
  81.3 10.8 %while.23 = (s32[]{:T(128)}, f32[8,128,256]{2,0,1:T(8,128)S(1)}, s32[3,8]{1,0:T(4,128)S(1)}, f32[3,8]{1,0:T(4,128)S(1)}, bf16[3,8,128,128]{2,3,1,0:T(8,128)(2,1)...) while((s32[]{:T(128)}, f32[8,128,256]{2,0,1:T(8,128)S(1)}, ...), condition=%wide.region_5.6_spmd.clone, body=%wide.region_4.5_spmd.clone.sunk | while | flops 92800152 | bytes 6033855 | solution.py:41
  81.3 0.6 gather_fusion.1
  81.9 1.2 fusion.69
  83.1 1.7 %convolution_add_fusion.5 = f32[8,128,256]{2,0,1:T(8,128)S(1)} fusion(f32[8,128,256]{2,1,0:T(8,128)S(1)} %fusion.69, f32[8,128,256]{2,0,1:T(8,128)S(1)} %get-tuple-element.287, pred[]{:T(512)S(6)} %compare.7, f32[8]{0:T(128)S(1)} %fusion.70, s32[8]{0:T(128)S(1)} %fusion.71), kind=kOutput, calls=%fused_computation.24.clone.1 | convolution fusion | flops 25690240 | bytes 3145793 | tf_op jit(solution)/shard_map/while/body/eval_jaxpr/bg,gif->bif/dot_general | solution.py:35
  84.9 0.6 gather_fusion.1
  85.5 1.2 fusion.69
  86.7 1.7 %convolution_add_fusion.5 = f32[8,128,256]{2,0,1:T(8,128)S(1)} fusion(f32[8,128,256]{2,1,0:T(8,128)S(1)} %fusion.69, f32[8,128,256]{2,0,1:T(8,128)S(1)} %get-tuple-element.287, pred[]{:T(512)S(6)} %compare.7, f32[8]{0:T(128)S(1)} %fusion.70, s32[8]{0:T(128)S(1)} %fusion.71), kind=kOutput, calls=%fused_computation.24.clone.1 | convolution fusion | flops 25690240 | bytes 3145793 | tf_op jit(solution)/shard_map/while/body/eval_jaxpr/bg,gif->bif/dot_general | solution.py:35
  89.1 1.2 fusion.69
  90.3 1.7 %convolution_add_fusion.5 = f32[8,128,256]{2,0,1:T(8,128)S(1)} fusion(f32[8,128,256]{2,1,0:T(8,128)S(1)} %fusion.69, f32[8,128,256]{2,0,1:T(8,128)S(1)} %get-tuple-element.287, pred[]{:T(512)S(6)} %compare.7, f32[8]{0:T(128)S(1)} %fusion.70, s32[8]{0:T(128)S(1)} %fusion.71), kind=kOutput, calls=%fused_computation.24.clone.1 | convolution fusion | flops 25690240 | bytes 3145793 | tf_op jit(solution)/shard_map/while/body/eval_jaxpr/bg,gif->bif/dot_general | solution.py:35
  92.3 28.2 %all_to_all.5 = bf16[8,128,256]{2,1,0:T(8,128)(2,1)S(1)} all-to-all(bf16[8,128,256]{2,1,0:T(8,128)(2,1)S(1)} %copy.24), channel_id=1, replica_groups=mesh['row'=8,'rep'=4] {'row'}, dimensions={0} | all-to-all | bytes 1048576 | tf_op jit(solution)/shard_map/all_to_all | solution.py:80
  120.5 0.7 convert_reduce_fusion
  121.2 32.9 %all-gather.3.cloned.1.call-done = f32[8192,256]{1,0:T(8,128)} async-done(((f32[256,256]{1,0:T(8,128)}), f32[8192,256]{1,0:T(8,128)}) %all-gather.3.cloned.1.call-update) | async-done | bytes 8388624 | tf_op jit(solution)/shard_map/all_gather | solution.py:75
  154.1 4.6 %reduce_sum.18 = f32[256,256]{1,0:T(8,128)} reduce(f32[32,256,256]{2,1,0:T(8,128)} %bitcast.82, f32[]{:T(128)} %constant.38.clone.1), dimensions={0}, to_apply=%region_3.4 | reduce | flops 2031616 | bytes 8650756 | tf_op jit(solution)/shard_map/reduce_sum | solution.py:75
  (41 shorter events, 2.1 us)
Async XLA Ops:
  7.2 58.0 %copy-start = (bf16[256,256]{1,0:T(8,128)(2,1)S(1)}, bf16[256,256]{1,0:T(8,128)(2,1)}, u32[]{:S(2)}) copy-start(bf16[256,256]{1,0:T(8,128)(2,1)} %param.12) | copy-start | bytes 393220
  7.2 57.9 %reduce-scatter.2.cloned.1.call-start = ((), (), s32[]{:S(2)}) async-start(), calls=%async_computation.2 | async-start | bytes 327680 | tf_op jit(solution)/shard_map/reduce_scatter | solution.py:63
  27.9 37.2 %copy-start.1 = (bf16[128,256]{1,0:T(8,128)(2,1)S(1)}, bf16[128,256]{1,0:T(8,128)(2,1)}, u32[]{:S(2)}) copy-start(bf16[128,256]{1,0:T(8,128)(2,1)} %param.13) | copy-start | bytes 196612
  39.6 114.5 %all-gather.3.cloned.1.call-start = ((), (), s32[]{:S(2)}) async-start(), calls=%async_computation.3 | async-start | bytes 8650752 | tf_op jit(solution)/shard_map/all_gather | solution.py:75
Sparse Core Ops, SparseCore 0:
  39.7 25.4 reduce-scatter.1
  68.7 85.3 all-gather.2
